TPU v7x, 512 devices: a whole 4x4x16 slice. The times are simulated.
512 devices in a mesh: dp: 32 (over z, x_hi), mp: 16 (over x_lo, y, core).
Axes of the slice: x: 4 (x_hi: 2, x_lo: 2; x = x_hi * 2 + x_lo), y: 4, z: 16, core: 2. Of those that a mesh axis runs over, the one named last changes fastest.
Arguments:
- tokens: bfloat16 [32768, 2048], P('dp', 'mp'), may hold values from -6 to 6
- norm_gain: bfloat16 [2048], replicated, may hold values from 0.099609375 to 1.8984375
- wi_gate: bfloat16 [2048, 5120], P(None, 'mp'), may hold values from -0.125 to 0.125
- wi_linear: bfloat16 [2048, 5120], P(None, 'mp'), may hold values from -0.125 to 0.125
- wo_out: bfloat16 [5120, 2048], P('mp'), may hold values from -0.078125 to 0.078125
- task_table: float32 [8, 64], replicated, may hold values from -5 to 5
- layer_table: float32 [24, 64], replicated, may hold values from -5 to 5
- task_ids: int32 [256], P('dp'), may hold values from 0 to 7
- layer_index: int32 [1], replicated, may hold values from 0 to 23
- hyper_in: bfloat16 [128, 1024], P(None, 'mp'), may hold values from -0.5 to 0.5
- gen_down: bfloat16 [1024, 131072], P(None, ('mp', 'dp')), may hold values from -0.0078125 to 0.0078125
- gen_up: bfloat16 [1024, 131072], P(None, ('mp', 'dp')), may hold values from -0.046875 to 0.046875
Outputs:
- mixed: bfloat16 [32768, 2048], P('dp', 'mp')
All inputs are finite; a program needn't handle non-finite values.
Results may differ from a plain program's by a relative error of at most 0.019.
Values may be sent and summed in bfloat16 or wider, within the bound.
No kernel may reach another device: no remote copies, remote signals or barrier semaphores. Data moves between devices by JAX's collectives and lax.ppermute only.
A program may use at most 64 MiB of HBM per device.

v0:
```python
import jax
import jax.numpy as jnp
from jax import lax
from jax.sharding import PartitionSpec as P

R = 64


def laid_out(blocks, dim):
    lengths = list(blocks.shape[1:])
    lengths[dim] *= blocks.shape[0]
    return jnp.moveaxis(blocks, 0, dim).reshape(lengths)


def from_everyone(shard, axis):
    copies = jnp.broadcast_to(shard, (lax.axis_size(axis), *shard.shape))
    return lax.all_to_all(copies, axis, split_axis=0, concat_axis=0, tiled=True)


def gather_directly(shard, axis, dim):
    return laid_out(from_everyone(shard, axis), dim)


def of_everyone(shard, axis):
    everything = from_everyone(shard, axis)
    return jnp.sum(everything.astype(jnp.float32), axis=0)


def matmul(left, right):
    return jnp.dot(left, right, preferred_element_type=jnp.float32)


def per_device(
    tokens,
    norm_gain,
    wi_gate,
    wi_linear,
    wo_out,
    task_table,
    layer_table,
    task_ids,
    layer_index,
    hyper_in,
    gen_down,
    gen_up,
):
    task_count = task_table.shape[0]
    layer_row = jnp.take(layer_table, layer_index, axis=0)
    embed = jnp.concatenate(
        [task_table, jnp.broadcast_to(layer_row, (task_count, layer_row.shape[1]))], axis=1
    ).astype(jnp.bfloat16)
    hidden_part = jnp.maximum(matmul(embed, hyper_in), 0.0).astype(jnp.bfloat16)
    hidden = gather_directly(hidden_part, "mp", 1)
    every_id = gather_directly(task_ids, "dp", 0)
    wanted = jnp.take(hidden, every_id, axis=0)
    made = (
        matmul(wanted, gen_down).astype(jnp.bfloat16),
        matmul(wanted, gen_up).astype(jnp.bfloat16),
    )
    local_down, local_up = (
        lax.all_to_all(made[0], "dp", split_axis=0, concat_axis=1, tiled=True),
        lax.all_to_all(made[1], "dp", split_axis=0, concat_axis=1, tiled=True),
    )
    full_rows = lax.all_gather(tokens, "mp", axis=1, tiled=True)
    wide = full_rows.astype(jnp.float32)
    scale = lax.rsqrt(jnp.mean(wide * wide, axis=-1, keepdims=True) + 1e-06)
    normed = (wide * scale * norm_gain.astype(jnp.float32)).astype(jnp.bfloat16)
    gate = matmul(normed, wi_gate)
    linear = matmul(normed, wi_linear)
    act = (jax.nn.gelu(gate, approximate=True) * linear).astype(jnp.bfloat16)
    seqs_dev = task_ids.shape[0]
    tok_dev = tokens.shape[0]
    seq_len = tok_dev // seqs_dev
    partial_sums = matmul(act, wo_out)
    ffout = lax.psum_scatter(
        partial_sums.astype(jnp.bfloat16), "mp", scatter_dimension=1, tiled=True
    )
    down_block = local_down.reshape(seqs_dev, -1, R)
    up_block = local_up.reshape(seqs_dev, -1, R)
    blocks = ffout.reshape(seqs_dev, seq_len, -1)
    squeeze_part = jnp.einsum(
        "std,sdr->str", blocks, down_block, preferred_element_type=jnp.float32
    )
    squeeze_full = of_everyone(squeeze_part.astype(jnp.bfloat16), "mp").astype(jnp.float32)
    squeezed = jnp.maximum(squeeze_full, 0.0).astype(jnp.bfloat16)
    expand = jnp.einsum("str,sdr->std", squeezed, up_block, preferred_element_type=jnp.float32)
    total = tokens.astype(jnp.float32) + ffout.astype(jnp.float32) + expand.reshape(tok_dev, -1)
    return total.astype(jnp.bfloat16)


def solution(mesh):
    return jax.shard_map(
        per_device,
        mesh=mesh,
        in_specs=(
            P("dp", "mp"),
            P(),
            P(None, "mp"),
            P(None, "mp"),
            P("mp", None),
            P(),
            P(),
            P("dp"),
            P(),
            P(None, "mp"),
            P(None, ("mp", "dp")),
            P(None, ("mp", "dp")),
        ),
        out_specs=P("dp", "mp"),
        check_vma=False,
    )
```

profile of v0, /device:TPU:25, one launch (start us, length us, event | category | flops | bytes accessed | tf_op | source)
XLA Modules:
  0.0 219.2 jit_solution(13709303609028139173)
XLA Ops:
  8.0 58.1 %all-gather.2.cloned.1.call-done = bf16[1024,2048]{1,0:T(8,128)(2,1)} async-done(((bf16[1024,128]{1,0:T(8,128)(2,1)}), bf16[1024,2048]{1,0:T(8,128)(2,1)}) %all-gather.2.cloned.1.call-update) | async-done | bytes 4194320 | tf_op jit(solution)/shard_map/all_gather | solution.py:64
  66.1 3.2 %fusion = f32[1024]{0:T(1024)S(1)} fusion(bf16[1024,2048]{1,0:T(8,128)(2,1)} %all-gather.2.cloned.1.call-done), kind=kLoop, calls=%fused_computation.3 | loop fusion | flops 6290432 | bytes 4198400 | tf_op jit(solution)/shard_map/reduce_sum | solution.py:66
  69.5 4.2 %fusion.12 = f32[1024,320]{0,1:T(8,128)} fusion(bf16[2048,320]{0,1:T(8,128)(2,1)} %param.14, bf16[1024,2048]{1,0:T(8,128)(2,1)S(1)} %copy-done.1, f32[2048]{0:T(1024)S(1)} %convert_element_type.45, f32[1024]{0:T(1024)S(1)} %add_rsqrt_fusion), kind=kOutput, calls=%fused_computation.18 | convolution fusion | flops 1350565888 | bytes 6828032 | tf_op jit(solution)/shard_map/dot_general | solution.py:30
  73.8 8.6 %convolution_convert_fusion = bf16[1024,2048]{1,0:T(8,128)(2,1)} fusion(bf16[320,2048]{1,0:T(8,128)(2,1)S(1)} %copy-done, bf16[2048,320]{0,1:T(8,128)(2,1)S(1)} %copy-done.10, f32[1024,320]{0,1:T(8,128)} %fusion.12, bf16[1024,2048]{1,0:T(8,128)(2,1)} %all-gather.2.cloned.1.call-done, f32[2048]{0:T(1024)S(1)} %convert_element_type.45, f32[1024]{0:T(1024)S(1)} %add_rsqrt_fusion), kind=kOutput, calls=%fused_computation.7 | convolution fusion | flops 2698117120 | bytes 12333056 | tf_op jit(solution)/shard_map/dot_general | solution.py:30
  82.4 6.4 %copy.23 = bf16[1024,2048]{0,1:T(8,128)(2,1)} copy(bf16[1024,2048]{1,0:T(8,128)(2,1)} %convolution_convert_fusion) | data formatting | bytes 8388608
  90.0 14.2 %all-to-all-start = ((s32[32,1,8]{2,1,0:T(1,128)}), s32[32,1,8]{2,1,0:T(1,128)S(1)}, u32[]{:S(2)}, u32[]{:S(2)}) async-start(s32[32,1,8]{2,1,0:T(1,128)} %broadcast_in_dim.38), calls=%async_computation | async-start | bytes 32768 | tf_op jit(solution)/shard_map/all_to_all | solution.py:17
  106.6 11.3 %all-to-all-done = s32[32,1,8]{2,1,0:T(1,128)S(1)} async-done(((s32[32,1,8]{2,1,0:T(1,128)}), s32[32,1,8]{2,1,0:T(1,128)S(1)}, u32[]{:S(2)}, u32[]{:S(2)}) %all-to-all-start) | async-done | bytes 1056 | tf_op jit(solution)/shard_map/all_to_all | solution.py:17
  117.9 6.1 %all-to-all-start.1 = ((bf16[16,2,256]{2,1,0:T(2,128)(2,1)}), bf16[16,2,256]{2,1,0:T(2,128)(2,1)S(1)}, u32[]{:S(2)}, u32[]{:S(2)}) async-start(bf16[16,2,256]{2,1,0:T(2,128)(2,1)} %reshape.145), calls=%async_computation.1 | async-start | bytes 32768 | tf_op jit(solution)/shard_map/all_to_all | solution.py:17
  125.6 2.6 %all-to-all-done.1 = bf16[16,2,256]{2,1,0:T(2,128)(2,1)S(1)} async-done(((bf16[16,2,256]{2,1,0:T(2,128)(2,1)}), bf16[16,2,256]{2,1,0:T(2,128)(2,1)S(1)}, u32[]{:S(2)}, u32[]{:S(2)}) %all-to-all-start.1) | async-done | bytes 16416 | tf_op jit(solution)/shard_map/all_to_all | solution.py:17
  128.4 1.2 gather_fusion
  129.6 1.0 fusion.14
  130.6 3.8 %all-to-all-start.2 = ((bf16[32,8,256]{2,1,0:T(8,128)(2,1)}), bf16[32,8,256]{2,1,0:T(8,128)(2,1)S(1)}, u32[]{:S(2)}, u32[]{:S(2)}) async-start(bf16[32,8,256]{2,1,0:T(8,128)(2,1)} %fusion.14), calls=%async_computation.2 | async-start | bytes 262144 | tf_op jit(solution)/shard_map/all_to_all | solution.py:61
  134.4 1.0 fusion.15
  135.4 14.6 %all-to-all-done.2 = bf16[32,8,256]{2,1,0:T(8,128)(2,1)S(1)} async-done(((bf16[32,8,256]{2,1,0:T(8,128)(2,1)}), bf16[32,8,256]{2,1,0:T(8,128)(2,1)S(1)}, u32[]{:S(2)}, u32[]{:S(2)}) %all-to-all-start.2) | async-done | bytes 131104 | tf_op jit(solution)/shard_map/all_to_all | solution.py:61
  150.0 5.2 %all-to-all-start.4 = ((bf16[32,8,256]{2,1,0:T(8,128)(2,1)}), bf16[32,8,256]{2,1,0:T(8,128)(2,1)S(1)}, u32[]{:S(2)}, u32[]{:S(2)}) async-start(bf16[32,8,256]{2,1,0:T(8,128)(2,1)} %fusion.15), calls=%async_computation.4 | async-start | bytes 262144 | tf_op jit(solution)/shard_map/all_to_all | solution.py:62
  155.4 7.9 %reduce-scatter.4.cloned.1.call-done = bf16[128,1024]{1,0:T(8,128)(2,1)} async-done(((bf16[2048,1024]{1,0:T(8,128)(2,1)}), bf16[128,1024]{1,0:T(8,128)(2,1)}) %reduce-scatter.4.cloned.1.call-update) | async-done | bytes 262160
  163.4 1.1 copy.24
  164.8 5.2 %all-to-all-done.4 = bf16[32,8,256]{2,1,0:T(8,128)(2,1)S(1)} async-done(((bf16[32,8,256]{2,1,0:T(8,128)(2,1)}), bf16[32,8,256]{2,1,0:T(8,128)(2,1)S(1)}, u32[]{:S(2)}, u32[]{:S(2)}) %all-to-all-start.4) | async-done | bytes 131104 | tf_op jit(solution)/shard_map/all_to_all | solution.py:62
  170.0 1.9 broadcast_in_dim.46
  171.9 8.9 %all-to-all-start.3 = ((bf16[16,8,128,64]{2,3,1,0:T(8,128)(2,1)}), bf16[16,8,128,64]{2,3,1,0:T(8,128)(2,1)S(1)}, u32[]{:S(2)}, u32[]{:S(2)}) async-start(bf16[16,8,128,64]{2,3,1,0:T(8,128)(2,1)} %broadcast_in_dim.46), calls=%async_computation.3 | async-start | bytes 4194304 | tf_op jit(solution)/shard_map/all_to_all | solution.py:17
  180.8 0.9 copy.19
  181.7 0.9 reshape.93
  182.6 27.8 %all-to-all-done.3 = bf16[16,8,128,64]{2,3,1,0:T(8,128)(2,1)S(1)} async-done(((bf16[16,8,128,64]{2,3,1,0:T(8,128)(2,1)}), bf16[16,8,128,64]{2,3,1,0:T(8,128)(2,1)S(1)}, u32[]{:S(2)}, u32[]{:S(2)}) %all-to-all-start.3) | async-done | bytes 2097184 | tf_op jit(solution)/shard_map/all_to_all | solution.py:17
  211.6 0.8 fusion.23
  (54 shorter events, 8.0 us)
Async XLA Ops:
  6.5 67.2 %copy-start = (bf16[320,2048]{1,0:T(8,128)(2,1)S(1)}, bf16[320,2048]{1,0:T(8,128)(2,1)}, u32[]{:S(2)}) copy-start(bf16[320,2048]{1,0:T(8,128)(2,1)} %param.16) | copy-start | bytes 3932164
  6.5 59.6 %all-gather.2.cloned.1.call-start = ((), (), s32[]{:S(2)}) async-start(), calls=%async_computation.6 | async-start | bytes 4456448 | tf_op jit(solution)/shard_map/all_gather | solution.py:64
  7.3 156.1 %reduce-scatter.4.cloned.1.call-start = ((), (), s32[]{:S(2)}) async-start(), calls=%async_computation.7 | async-start | bytes 4456448
  66.1 3.4 %copy-start.1 = (bf16[1024,2048]{1,0:T(8,128)(2,1)S(1)}, bf16[1024,2048]{1,0:T(8,128)(2,1)}, u32[]{:S(2)}) copy-start(bf16[1024,2048]{1,0:T(8,128)(2,1)} %all-gather.2.cloned.1.call-done) | copy-start | bytes 12582916
  69.5 4.2 %copy-start.10 = (bf16[2048,320]{0,1:T(8,128)(2,1)S(1)}, bf16[2048,320]{0,1:T(8,128)(2,1)}, u32[]{:S(2)}) copy-start(bf16[2048,320]{0,1:T(8,128)(2,1)} %param.15) | copy-start | bytes 3932164
  88.8 0.7 copy-start.9
  88.8 16.2 %copy-start.8 = (f32[8,64]{1,0:T(8,128)S(1)}, f32[8,64]{1,0:T(8,128)}, u32[]{:S(2)}) copy-start(f32[8,64]{1,0:T(8,128)} %param.17) | copy-start | bytes 6148
  88.8 17.0 %copy-start.7 = (bf16[128,64]{0,1:T(8,128)(2,1)S(1)}, bf16[128,64]{0,1:T(8,128)(2,1)}, u32[]{:S(2)}) copy-start(bf16[128,64]{0,1:T(8,128)(2,1)} %param.21) | copy-start | bytes 49156
  90.0 27.9 %all-to-all-start = ((s32[32,1,8]{2,1,0:T(1,128)}), s32[32,1,8]{2,1,0:T(1,128)S(1)}, u32[]{:S(2)}, u32[]{:S(2)}) async-start(s32[32,1,8]{2,1,0:T(1,128)} %broadcast_in_dim.38), calls=%async_computation | async-start | bytes 32768 | tf_op jit(solution)/shard_map/all_to_all | solution.py:17
  117.9 10.2 %all-to-all-start.1 = ((bf16[16,2,256]{2,1,0:T(2,128)(2,1)}), bf16[16,2,256]{2,1,0:T(2,128)(2,1)S(1)}, u32[]{:S(2)}, u32[]{:S(2)}) async-start(bf16[16,2,256]{2,1,0:T(2,128)(2,1)} %reshape.145), calls=%async_computation.1 | async-start | bytes 32768 | tf_op jit(solution)/shard_map/all_to_all | solution.py:17
  128.4 1.2 copy-start.11
  129.6 4.9 %copy-start.12 = (bf16[1024,256]{1,0:T(8,128)(2,1)S(1)}, bf16[1024,256]{1,0:T(8,128)(2,1)}, u32[]{:S(2)}) copy-start(bf16[1024,256]{1,0:T(8,128)(2,1)} %param.23) | copy-start | bytes 1572868
  130.6 19.4 %all-to-all-start.2 = ((bf16[32,8,256]{2,1,0:T(8,128)(2,1)}), bf16[32,8,256]{2,1,0:T(8,128)(2,1)S(1)}, u32[]{:S(2)}, u32[]{:S(2)}) async-start(bf16[32,8,256]{2,1,0:T(8,128)(2,1)} %fusion.14), calls=%async_computation.2 | async-start | bytes 262144 | tf_op jit(solution)/shard_map/all_to_all | solution.py:61
  150.0 20.0 %all-to-all-start.4 = ((bf16[32,8,256]{2,1,0:T(8,128)(2,1)}), bf16[32,8,256]{2,1,0:T(8,128)(2,1)S(1)}, u32[]{:S(2)}, u32[]{:S(2)}) async-start(bf16[32,8,256]{2,1,0:T(8,128)(2,1)} %fusion.15), calls=%async_computation.4 | async-start | bytes 262144 | tf_op jit(solution)/shard_map/all_to_all | solution.py:62
  164.5 7.4 %copy-start.2 = (bf16[1024,128]{1,0:T(8,128)(2,1)}, bf16[1024,128]{1,0:T(8,128)(2,1)S(1)}, u32[]{:S(2)}) copy-start(bf16[1024,128]{1,0:T(8,128)(2,1)S(1)} %copy.24) | copy-start | bytes 786436
  170.0 1.9 copy-start.6
  171.9 38.4 %all-to-all-start.3 = ((bf16[16,8,128,64]{2,3,1,0:T(8,128)(2,1)}), bf16[16,8,128,64]{2,3,1,0:T(8,128)(2,1)S(1)}, u32[]{:S(2)}, u32[]{:S(2)}) async-start(bf16[16,8,128,64]{2,3,1,0:T(8,128)(2,1)} %broadcast_in_dim.46), calls=%async_computation.3 | async-start | bytes 4194304 | tf_op jit(solution)/shard_map/all_to_all | solution.py:17
  210.3 1.0 copy-start.5
  210.3 1.3 copy-start.3
  210.3 1.3 copy-start.4
Sparse Core Ops, SparseCore 0:
  9.4 56.6 all-gather.1
  88.9 74.3 reduce-scatter.3
where the time goes:
time: 220 us; the launch traced here: 219 us
  waiting for transfers between devices  128 us (58%)
  starting transfers between devices  38.3 us (17%)
  local copies, waits for them, and re-layouts  16.4 us (7%)
  matrix products  15.6 us (7%)
  between operations  14.2 us (6%)
  other arithmetic  6.5 us (3%)
    all_gather x1, waiting for transfers between devices, per_device(): full_rows = lax.all_gather(tokens, 'mp', axis=1, tiled=True)  58.1 us
    all_to_all x3, waiting for transfers between devices, from_everyone(): return lax.all_to_all(copies, axis, split_axis=0, concat_axis=0, tiled=True)  41.7 us
    all_to_all x3, starting transfers between devices, from_everyone(): return lax.all_to_all(copies, axis, split_axis=0, concat_axis=0, tiled=True)  29.2 us
    dot_general x5, matrix products, matmul(): return jnp.dot(left, right, preferred_element_type=jnp.float32)  15 us
    all_to_all x1, waiting for transfers between devices, per_device(): lax.all_to_all(made[0], 'dp', split_axis=0, concat_axis=1, tiled=True)  14.6 us
    unnamed x30, local copies, waits for them, and re-layouts  9.83 us
    unnamed x3, waiting for transfers between devices  8.67 us
    all_to_all x1, starting transfers between devices, per_device(): lax.all_to_all(made[1], 'dp', split_axis=0, concat_axis=1, tiled=True)  5.21 us
  transfers between devices with their start and end apart: 7, of which 7 were waited for; matrix products, arithmetic and copies ran while one was open for 5% of the time, Pallas kernels for 0%

commit v1 on v0

--- a/solution.py
+++ b/solution.py
@@ -61,7 +61,9 @@
         lax.all_to_all(made[0], "dp", split_axis=0, concat_axis=1, tiled=True),
         lax.all_to_all(made[1], "dp", split_axis=0, concat_axis=1, tiled=True),
     )
-    full_rows = lax.all_gather(tokens, "mp", axis=1, tiled=True)
+    full_rows = jnp.concatenate(
+        lax.all_to_all(jnp.stack([tokens for _ in range(lax.psum(1, "mp"))]), "mp", 0, 0), 1
+    )
     wide = full_rows.astype(jnp.float32)
     scale = lax.rsqrt(jnp.mean(wide * wide, axis=-1, keepdims=True) + 1e-06)
     normed = (wide * scale * norm_gain.astype(jnp.float32)).astype(jnp.bfloat16)

time: 220 us -> 238 us (1.082)
  starting transfers between devices: 38.3 us -> 48.2 us
  local copies, waits for them, and re-layouts: 16.4 us -> 21.8 us
  waiting for transfers between devices: 128 us -> 131 us
    all_to_all x0 -> x1, waiting for transfers between devices: none -> 61.5 us  [per_device(): lax.all_to_all(jnp.stack([tokens for _ in range(lax.psum(1, 'mp'))]), 'mp...]
    all_gather x1 -> x0, waiting for transfers between devices: 58.1 us -> none  [per_device(): full_rows = lax.all_gather(tokens, 'mp', axis=1, tiled=True)]
    all_to_all x0 -> x1, starting transfers between devices: none -> 10.3 us  [per_device(): lax.all_to_all(jnp.stack([tokens for _ in range(lax.psum(1, 'mp'))]), 'mp...]
    unnamed x30 -> x35, local copies, waits for them, and re-layouts: 9.83 us -> 12.8 us
    another operation x0 -> x1, local copies, waits for them, and re-layouts: none -> 2.52 us  [per_device(): jnp.stack([tokens for _ in range(lax.psum(1, 'mp'))])]
    unnamed x3 -> x2, waiting for transfers between devices: 8.67 us -> 7.69 us
  transfers between devices with their start and end apart: 7 -> 7, of which waited for: 7 -> 7; matrix products, arithmetic and copies ran while one was open for 5% -> 4% of each run, Pallas kernels for 0% -> 0%
where the time goes in v1:
time: 238 us; the launch traced here: 237 us
  waiting for transfers between devices  131 us (55%)
  starting transfers between devices  48.2 us (20%)
  local copies, waits for them, and re-layouts  21.8 us (9%)
  between operations  14.3 us (6%)
  matrix products  13.9 us (6%)
  other arithmetic  8.45 us (4%)
    all_to_all x1, waiting for transfers between devices, per_device(): lax.all_to_all(jnp.stack([tokens for _ in range(lax.psum(1, 'mp'))]), 'mp...  61.5 us
    all_to_all x3, waiting for transfers between devices, from_everyone(): return lax.all_to_all(copies, axis, split_axis=0, concat_axis=0, tiled=True)  41.8 us
    all_to_all x3, starting transfers between devices, from_everyone(): return lax.all_to_all(copies, axis, split_axis=0, concat_axis=0, tiled=True)  28.3 us
    all_to_all x1, waiting for transfers between devices, per_device(): lax.all_to_all(made[0], 'dp', split_axis=0, concat_axis=1, tiled=True)  14.1 us
    dot_general x5, matrix products, matmul(): return jnp.dot(left, right, preferred_element_type=jnp.float32)  13.3 us
    unnamed x35, local copies, waits for them, and re-layouts  12.8 us
    all_to_all x1, starting transfers between devices, per_device(): lax.all_to_all(jnp.stack([tokens for _ in range(lax.psum(1, 'mp'))]), 'mp...  10.3 us
    unnamed x2, waiting for transfers between devices  7.69 us
  transfers between devices with their start and end apart: 7, of which 7 were waited for; matrix products, arithmetic and copies ran while one was open for 4% of the time, Pallas kernels for 0%

profile of v1, /device:TPU:25, one launch (start us, length us, event | category | flops | bytes accessed | tf_op | source)
XLA Modules:
  0.0 237.1 jit_solution(6015576309951389350)
XLA Ops:
  6.5 1.2 copy.17
  7.7 2.5 %stack.2 = bf16[16,1024,128]{1,2,0:T(8,128)(2,1)} broadcast(bf16[1024,128]{0,1:T(8,128)(2,1)S(1)} %copy.17), dimensions={1,2} | broadcast | bytes 4456448 | tf_op jit(solution)/shard_map/stack | solution.py:65
  10.3 10.3 %all-to-all-start = ((bf16[16,1024,128]{1,2,0:T(8,128)(2,1)}), bf16[16,1024,128]{1,2,0:T(8,128)(2,1)}, u32[]{:S(2)}, u32[]{:S(2)}) async-start(bf16[16,1024,128]{1,2,0:T(8,128)(2,1)} %stack.2), calls=%async_computation | async-start | bytes 8388608 | tf_op jit(solution)/shard_map/all_to_all | solution.py:65
  20.7 61.5 %all-to-all-done = bf16[16,1024,128]{1,2,0:T(8,128)(2,1)} async-done(((bf16[16,1024,128]{1,2,0:T(8,128)(2,1)}), bf16[16,1024,128]{1,2,0:T(8,128)(2,1)}, u32[]{:S(2)}, u32[]{:S(2)}) %all-to-all-start) | async-done | bytes 4194336 | tf_op jit(solution)/shard_map/all_to_all | solution.py:65
  82.2 3.1 %multiply_reduce_fusion = f32[1024]{0:T(1024)S(1)} fusion(bf16[16,1024,128]{1,2,0:T(8,128)(2,1)} %all-to-all-done), kind=kLoop, calls=%fused_computation.4 | loop fusion | flops 6290432 | bytes 4198400 | tf_op jit(solution)/shard_map/reduce_sum | solution.py:68
  85.3 2.9 %fusion.1 = bf16[1024,2048]{0,1:T(8,128)(2,1)S(1)} fusion(f32[2048]{0:T(1024)S(1)} %convert_element_type.58, f32[1024]{0:T(1024)S(1)} %add_rsqrt_fusion, bf16[16,1024,128]{1,2,0:T(8,128)(2,1)} %all-to-all-done), kind=kLoop, calls=%fused_computation.3 | loop fusion | flops 8388608 | bytes 8400896 | tf_op jit(solution)/shard_map/convert_element_type | solution.py:69
  88.2 1.9 copy-done.1
  90.2 2.7 %fusion.33 = f32[1024,320]{0,1:T(8,128)} fusion(bf16[2048,320]{0,1:T(8,128)(2,1)S(1)} %copy-done.11, bf16[1024,2048]{0,1:T(8,128)(2,1)S(1)} %fusion.1), kind=kOutput, calls=%fused_computation.53 | convolution fusion | flops 1342177280 | bytes 6815744 | tf_op jit(solution)/shard_map/dot_general | solution.py:30
  92.9 8.4 %convolution_convert_fusion = bf16[1024,2048]{1,0:T(8,128)(2,1)} fusion(bf16[320,2048]{1,0:T(8,128)(2,1)S(1)} %copy-done, bf16[2048,320]{0,1:T(8,128)(2,1)S(1)} %copy-done.12, bf16[1024,2048]{0,1:T(8,128)(2,1)} %copy-done.1, f32[1024,320]{0,1:T(8,128)} %fusion.33), kind=kOutput, calls=%fused_computation.6 | convolution fusion | flops 2689728512 | bytes 12320768 | tf_op jit(solution)/shard_map/dot_general | solution.py:30
  101.3 6.4 %copy.25 = bf16[1024,2048]{0,1:T(8,128)(2,1)} copy(bf16[1024,2048]{1,0:T(8,128)(2,1)} %convolution_convert_fusion) | data formatting | bytes 8388608
  109.0 13.1 %all-to-all-start.1 = ((s32[32,1,8]{2,1,0:T(1,128)}), s32[32,1,8]{2,1,0:T(1,128)S(1)}, u32[]{:S(2)}, u32[]{:S(2)}) async-start(s32[32,1,8]{2,1,0:T(1,128)} %broadcast_in_dim.38), calls=%async_computation.1 | async-start | bytes 32768 | tf_op jit(solution)/shard_map/all_to_all | solution.py:17
  124.4 11.2 %all-to-all-done.1 = s32[32,1,8]{2,1,0:T(1,128)S(1)} async-done(((s32[32,1,8]{2,1,0:T(1,128)}), s32[32,1,8]{2,1,0:T(1,128)S(1)}, u32[]{:S(2)}, u32[]{:S(2)}) %all-to-all-start.1) | async-done | bytes 1056 | tf_op jit(solution)/shard_map/all_to_all | solution.py:17
  135.7 6.3 %all-to-all-start.2 = ((bf16[16,2,256]{2,1,0:T(2,128)(2,1)}), bf16[16,2,256]{2,1,0:T(2,128)(2,1)S(1)}, u32[]{:S(2)}, u32[]{:S(2)}) async-start(bf16[16,2,256]{2,1,0:T(2,128)(2,1)} %reshape.152), calls=%async_computation.2 | async-start | bytes 32768 | tf_op jit(solution)/shard_map/all_to_all | solution.py:17
  143.3 2.8 %all-to-all-done.2 = bf16[16,2,256]{2,1,0:T(2,128)(2,1)S(1)} async-done(((bf16[16,2,256]{2,1,0:T(2,128)(2,1)}), bf16[16,2,256]{2,1,0:T(2,128)(2,1)S(1)}, u32[]{:S(2)}, u32[]{:S(2)}) %all-to-all-start.2) | async-done | bytes 16416 | tf_op jit(solution)/shard_map/all_to_all | solution.py:17
  146.3 1.2 gather_fusion
  148.5 3.9 %all-to-all-start.3 = ((bf16[32,8,256]{2,1,0:T(8,128)(2,1)}), bf16[32,8,256]{2,1,0:T(8,128)(2,1)S(1)}, u32[]{:S(2)}, u32[]{:S(2)}) async-start(bf16[32,8,256]{2,1,0:T(8,128)(2,1)} %fusion.10), calls=%async_computation.3 | async-start | bytes 262144 | tf_op jit(solution)/shard_map/all_to_all | solution.py:61
  153.3 14.1 %all-to-all-done.3 = bf16[32,8,256]{2,1,0:T(8,128)(2,1)S(1)} async-done(((bf16[32,8,256]{2,1,0:T(8,128)(2,1)}), bf16[32,8,256]{2,1,0:T(8,128)(2,1)S(1)}, u32[]{:S(2)}, u32[]{:S(2)}) %all-to-all-start.3) | async-done | bytes 131104 | tf_op jit(solution)/shard_map/all_to_all | solution.py:61
  167.4 5.7 %all-to-all-start.5 = ((bf16[32,8,256]{2,1,0:T(8,128)(2,1)}), bf16[32,8,256]{2,1,0:T(8,128)(2,1)S(1)}, u32[]{:S(2)}, u32[]{:S(2)}) async-start(bf16[32,8,256]{2,1,0:T(8,128)(2,1)} %fusion.11), calls=%async_computation.5 | async-start | bytes 262144 | tf_op jit(solution)/shard_map/all_to_all | solution.py:62
  173.3 7.7 %reduce-scatter.4.cloned.1.call-done = bf16[128,1024]{1,0:T(8,128)(2,1)} async-done(((bf16[2048,1024]{1,0:T(8,128)(2,1)}), bf16[128,1024]{1,0:T(8,128)(2,1)}) %reduce-scatter.4.cloned.1.call-update) | async-done | bytes 262160
  181.0 1.1 copy.26
  182.4 5.5 %all-to-all-done.5 = bf16[32,8,256]{2,1,0:T(8,128)(2,1)S(1)} async-done(((bf16[32,8,256]{2,1,0:T(8,128)(2,1)}), bf16[32,8,256]{2,1,0:T(8,128)(2,1)S(1)}, u32[]{:S(2)}, u32[]{:S(2)}) %all-to-all-start.5) | async-done | bytes 131104 | tf_op jit(solution)/shard_map/all_to_all | solution.py:62
  187.9 1.9 broadcast_in_dim.46
  189.7 8.9 %all-to-all-start.4 = ((bf16[16,8,128,64]{2,3,1,0:T(8,128)(2,1)}), bf16[16,8,128,64]{2,3,1,0:T(8,128)(2,1)S(1)}, u32[]{:S(2)}, u32[]{:S(2)}) async-start(bf16[16,8,128,64]{2,3,1,0:T(8,128)(2,1)} %broadcast_in_dim.46), calls=%async_computation.4 | async-start | bytes 4194304 | tf_op jit(solution)/shard_map/all_to_all | solution.py:17
  200.4 27.8 %all-to-all-done.4 = bf16[16,8,128,64]{2,3,1,0:T(8,128)(2,1)S(1)} async-done(((bf16[16,8,128,64]{2,3,1,0:T(8,128)(2,1)}), bf16[16,8,128,64]{2,3,1,0:T(8,128)(2,1)S(1)}, u32[]{:S(2)}, u32[]{:S(2)}) %all-to-all-start.4) | async-done | bytes 2097184 | tf_op jit(solution)/shard_map/all_to_all | solution.py:17
  (60 shorter events, 10.8 us)
Async XLA Ops:
  6.5 86.4 %copy-start = (bf16[320,2048]{1,0:T(8,128)(2,1)S(1)}, bf16[320,2048]{1,0:T(8,128)(2,1)}, u32[]{:S(2)}) copy-start(bf16[320,2048]{1,0:T(8,128)(2,1)} %param.16) | copy-start | bytes 3932164
  10.3 10.4 %copy-start.8 = (bf16[2048]{0:T(1024)(128)(2,1)S(1)}, bf16[2048]{0:T(1024)(128)(2,1)}, u32[]{:S(2)}) copy-start(bf16[2048]{0:T(1024)(128)(2,1)} %param.13) | copy-start | bytes 12292
  10.3 72.0 %all-to-all-start = ((bf16[16,1024,128]{1,2,0:T(8,128)(2,1)}), bf16[16,1024,128]{1,2,0:T(8,128)(2,1)}, u32[]{:S(2)}, u32[]{:S(2)}) async-start(bf16[16,1024,128]{1,2,0:T(8,128)(2,1)} %stack.2), calls=%async_computation | async-start | bytes 8388608 | tf_op jit(solution)/shard_map/all_to_all | solution.py:65
  20.6 160.4 %reduce-scatter.4.cloned.1.call-start = ((), (), s32[]{:S(2)}) async-start(), calls=%async_computation.7 | async-start | bytes 4456448
  85.3 4.8 %copy-start.11 = (bf16[2048,320]{0,1:T(8,128)(2,1)S(1)}, bf16[2048,320]{0,1:T(8,128)(2,1)}, u32[]{:S(2)}) copy-start(bf16[2048,320]{0,1:T(8,128)(2,1)} %param.14) | copy-start | bytes 3932164
  88.2 2.0 copy-start.1
  90.2 2.7 %copy-start.12 = (bf16[2048,320]{0,1:T(8,128)(2,1)S(1)}, bf16[2048,320]{0,1:T(8,128)(2,1)}, u32[]{:S(2)}) copy-start(bf16[2048,320]{0,1:T(8,128)(2,1)} %param.15) | copy-start | bytes 3932164
  107.7 0.7 copy-start.10
  107.7 15.0 %copy-start.9 = (f32[8,64]{1,0:T(8,128)S(1)}, f32[8,64]{1,0:T(8,128)}, u32[]{:S(2)}) copy-start(f32[8,64]{1,0:T(8,128)} %param.17) | copy-start | bytes 6148
  107.7 15.8 %copy-start.7 = (bf16[128,64]{0,1:T(8,128)(2,1)S(1)}, bf16[128,64]{0,1:T(8,128)(2,1)}, u32[]{:S(2)}) copy-start(bf16[128,64]{0,1:T(8,128)(2,1)} %param.21) | copy-start | bytes 49156
  109.0 26.7 %all-to-all-start.1 = ((s32[32,1,8]{2,1,0:T(1,128)}), s32[32,1,8]{2,1,0:T(1,128)S(1)}, u32[]{:S(2)}, u32[]{:S(2)}) async-start(s32[32,1,8]{2,1,0:T(1,128)} %broadcast_in_dim.38), calls=%async_computation.1 | async-start | bytes 32768 | tf_op jit(solution)/shard_map/all_to_all | solution.py:17
  135.7 10.4 %all-to-all-start.2 = ((bf16[16,2,256]{2,1,0:T(2,128)(2,1)}), bf16[16,2,256]{2,1,0:T(2,128)(2,1)S(1)}, u32[]{:S(2)}, u32[]{:S(2)}) async-start(bf16[16,2,256]{2,1,0:T(2,128)(2,1)} %reshape.152), calls=%async_computation.2 | async-start | bytes 32768 | tf_op jit(solution)/shard_map/all_to_all | solution.py:17
  146.2 1.2 copy-start.13
  147.4 4.9 %copy-start.14 = (bf16[1024,256]{1,0:T(8,128)(2,1)S(1)}, bf16[1024,256]{1,0:T(8,128)(2,1)}, u32[]{:S(2)}) copy-start(bf16[1024,256]{1,0:T(8,128)(2,1)} %param.23) | copy-start | bytes 1572868
  148.5 19.0 %all-to-all-start.3 = ((bf16[32,8,256]{2,1,0:T(8,128)(2,1)}), bf16[32,8,256]{2,1,0:T(8,128)(2,1)S(1)}, u32[]{:S(2)}, u32[]{:S(2)}) async-start(bf16[32,8,256]{2,1,0:T(8,128)(2,1)} %fusion.10), calls=%async_computation.3 | async-start | bytes 262144 | tf_op jit(solution)/shard_map/all_to_all | solution.py:61
  167.4 20.4 %all-to-all-start.5 = ((bf16[32,8,256]{2,1,0:T(8,128)(2,1)}), bf16[32,8,256]{2,1,0:T(8,128)(2,1)S(1)}, u32[]{:S(2)}, u32[]{:S(2)}) async-start(bf16[32,8,256]{2,1,0:T(8,128)(2,1)} %fusion.11), calls=%async_computation.5 | async-start | bytes 262144 | tf_op jit(solution)/shard_map/all_to_all | solution.py:62
  182.1 7.6 %copy-start.2 = (bf16[1024,128]{1,0:T(8,128)(2,1)}, bf16[1024,128]{1,0:T(8,128)(2,1)S(1)}, u32[]{:S(2)}) copy-start(bf16[1024,128]{1,0:T(8,128)(2,1)S(1)} %copy.26) | copy-start | bytes 786436
  187.9 1.9 copy-start.6
  189.7 38.4 %all-to-all-start.4 = ((bf16[16,8,128,64]{2,3,1,0:T(8,128)(2,1)}), bf16[16,8,128,64]{2,3,1,0:T(8,128)(2,1)S(1)}, u32[]{:S(2)}, u32[]{:S(2)}) async-start(bf16[16,8,128,64]{2,3,1,0:T(8,128)(2,1)} %broadcast_in_dim.46), calls=%async_computation.4 | async-start | bytes 4194304 | tf_op jit(solution)/shard_map/all_to_all | solution.py:17
  228.2 1.0 copy-start.5
  228.2 1.3 copy-start.3
  228.2 1.3 copy-start.4
Sparse Core Ops, SparseCore 0:
  107.9 73.0 reduce-scatter.3
